TPU v7x, 512 devices: a whole 4x8x8 slice. The times are simulated.
512 devices in a mesh: head: 8 (over x, core), blk: 64 (over y, z).
Axes of the slice: x: 4, y: 8, z: 8, core: 2. Of those that a mesh axis runs over, the one named last changes fastest.
Arguments:
- suffix_hidden: bfloat16 [1536, 2048], P('blk'), may hold values from -400 to 400
- prefix_hidden: bfloat16 [16384, 2048], P('blk'), may hold values from -400 to 400
- kv_cache: bfloat16 [2, 16384, 8, 256], P(None, 'blk', 'head'), may hold values from -300 to 300
- norm_gain: float32 [2048], replicated, may hold values from 0.1 to 1.9
- norm_bias: float32 [2048], replicated, may hold values from -3 to 3
- qkv_weight: bfloat16 [2048, 8, 768], P('blk', 'head'), may hold values from -0.125 to 0.125
- qkv_bias: float32 [8, 768], P('head'), may hold values from -3 to 3
- out_weight: bfloat16 [8, 256, 2048], P('head', 'blk'), may hold values from -0.125 to 0.125
- out_bias: float32 [2048], replicated, may hold values from -3 to 3
- suffix_lengths: int32 [4], replicated, may hold values from 1 to 768, 1536 in all
- prefix_blocks: int32 [4], replicated, may hold values from 1 to 32, 64 in all
- block_owner: int32 [64], replicated, may hold values from 0 to 63, each once
- recompute_flag: int32 [16384], P('blk'), may hold values from 0 to 1, as said below
Outputs:
- attn_out: bfloat16 [1536, 2048], P('blk', 'head')
Inputs may be any that keep to these rules, and one draw needn't show every extreme that they name: `recompute_flag`: each storage block of 256 cache rows holds exactly 25 ones.
All inputs are finite; a program needn't handle non-finite values.
Results may differ from a plain program's by a relative error of at most 0.015.
Values may be sent and summed in bfloat16 or wider, within the bound.
A program may use at most 64 MiB of HBM per device.

v0:
```python
import math
import jax
import jax.numpy as jnp
from jax import lax
from jax.sharding import PartitionSpec as P

FLAG_DEV = 25
EPSILON = 1e-05
MASKED = -1e30


def layer_norm(states, norm_scale, norm_shift):
    widened = states.astype(jnp.float32)
    average = jnp.mean(widened, axis=-1, keepdims=True)
    center = widened - average
    variance = jnp.mean(center * center, axis=-1, keepdims=True)
    return (center * lax.rsqrt(variance + EPSILON) * norm_scale + norm_shift).astype(jnp.bfloat16)


def body(
    suffix_hidden,
    prefix_hidden,
    kv_cache,
    norm_gain,
    norm_bias,
    qkv_weight,
    qkv_bias,
    out_weight,
    out_bias,
    suffix_lengths,
    prefix_blocks,
    block_owner,
    recompute_flag,
):
    blk_total = lax.axis_size("blk")
    own_index = lax.axis_index("blk")
    row_count = suffix_hidden.shape[0]
    cache_rows = prefix_hidden.shape[0]
    heads_dev = qkv_weight.shape[1]
    head_dim = qkv_weight.shape[2] // 3
    total_rows = row_count * blk_total
    own_first = own_index * row_count
    tenant_ends = jnp.cumsum(suffix_lengths)
    row_ids = jnp.arange(total_rows, dtype=jnp.int32)
    row_tenant = jnp.sum((row_ids[:, None] >= tenant_ends[None, :]).astype(jnp.int32), axis=1)
    block_ends = jnp.cumsum(prefix_blocks)
    block_slots = jnp.arange(blk_total, dtype=jnp.int32)
    global_block = jnp.sum(jnp.where(block_owner == own_index, block_slots, 0))
    block_tenant = jnp.sum((global_block >= block_ends).astype(jnp.int32))
    normed = layer_norm(suffix_hidden, norm_gain, norm_bias)
    flagged = jnp.argsort(1 - recompute_flag, stable=True)[:FLAG_DEV]
    prefix_normed = layer_norm(prefix_hidden[flagged], norm_gain, norm_bias)
    qkv_rows = qkv_weight.shape[0]
    out_rows = out_weight.shape[1]
    model_dim = out_weight.shape[2]
    packed_weights = jnp.concatenate([qkv_weight.reshape(1, -1), out_weight.reshape(1, -1)], axis=1)
    fetched_all = lax.all_gather(packed_weights, "blk", axis=0, tiled=True)
    qkv_size = qkv_rows * heads_dev * 3 * head_dim
    fetched = fetched_all[:, :qkv_size].reshape(blk_total * qkv_rows, heads_dev, 3 * head_dim)
    out_fetched = fetched_all[:, qkv_size:].reshape(blk_total, heads_dev, out_rows, model_dim)
    out_fetched = jnp.transpose(out_fetched, (1, 0, 2, 3)).reshape(
        heads_dev, blk_total * out_rows, model_dim
    )
    piece_rows = fetched.shape[0]
    flattened = fetched.reshape(piece_rows, heads_dev * 3 * head_dim)
    kv_part = fetched[:, :, head_dim:].reshape(piece_rows, heads_dev * 2 * head_dim)
    suffix_acc = jnp.dot(normed, flattened, preferred_element_type=jnp.float32)
    prefix_acc = jnp.dot(prefix_normed, kv_part, preferred_element_type=jnp.float32)
    suffix_acc, prefix_acc = (suffix_acc, prefix_acc)
    projected = (
        (suffix_acc + qkv_bias.reshape(-1))
        .astype(jnp.bfloat16)
        .reshape(row_count, heads_dev, 3 * head_dim)
    )
    recomputed = (
        (prefix_acc + qkv_bias[:, head_dim:].reshape(-1))
        .astype(jnp.bfloat16)
        .reshape(FLAG_DEV, heads_dev, 2 * head_dim)
    )
    own_queries = projected[:, :, :head_dim].reshape(row_count, heads_dev * head_dim)
    gathered = lax.all_gather(own_queries, "blk", axis=0, tiled=True)
    prefix_keys = kv_cache[0].at[flagged].set(recomputed[:, :, :head_dim])
    prefix_values = kv_cache[1].at[flagged].set(recomputed[:, :, head_dim:])
    keys_all = jnp.concatenate([prefix_keys, projected[:, :, head_dim : 2 * head_dim]], axis=0)
    values_all = jnp.concatenate([prefix_values, projected[:, :, 2 * head_dim :]], axis=0)
    own_tenant = lax.dynamic_slice_in_dim(row_tenant, own_first, row_count, 0)
    key_tenant = jnp.concatenate([jnp.full((cache_rows,), block_tenant, jnp.int32), own_tenant])
    key_position = jnp.concatenate(
        [jnp.full((cache_rows,), -1, jnp.int32), own_first + jnp.arange(row_count, dtype=jnp.int32)]
    )
    scale = head_dim ** (-0.5)
    qblock = math.gcd(total_rows, 512)
    block_total = total_rows // qblock

    def partial_block(offset):
        query_block = lax.dynamic_slice_in_dim(gathered, offset, qblock, 0).reshape(
            qblock, heads_dev, head_dim
        )
        query_tenant = lax.dynamic_slice_in_dim(row_tenant, offset, qblock, 0)
        query_position = offset + jnp.arange(qblock, dtype=jnp.int32)
        allowed = (query_tenant[:, None] == key_tenant[None, :]) & (
            key_position[None, :] <= query_position[:, None]
        )
        scores = (
            jnp.einsum("qhd,khd->hqk", query_block, keys_all, preferred_element_type=jnp.float32)
            * scale
        )
        gate = allowed[None, :, :]
        row_peak = jnp.max(jnp.where(gate, scores, MASKED), axis=2)
        weights = jnp.where(gate, jnp.exp(scores - row_peak[:, :, None]), 0.0)
        denominator = jnp.sum(weights, axis=2)
        numerator = jnp.einsum(
            "hqk,khd->qhd",
            weights.astype(jnp.bfloat16),
            values_all,
            preferred_element_type=jnp.float32,
        )
        return (numerator.reshape(qblock, heads_dev * head_dim), denominator.T, row_peak.T)

    def fill_block(step_index, buffers):
        numer_buf, denom_buf, peak_buf = buffers
        offset = step_index * qblock
        numerator, denominator, row_peak = partial_block(offset)
        numer_buf = lax.dynamic_update_slice_in_dim(numer_buf, numerator, offset, 0)
        denom_buf = lax.dynamic_update_slice_in_dim(denom_buf, denominator, offset, 0)
        peak_buf = lax.dynamic_update_slice_in_dim(peak_buf, row_peak, offset, 0)
        return (numer_buf, denom_buf, peak_buf)

    initial = (
        jnp.zeros((total_rows, heads_dev * head_dim), jnp.float32),
        jnp.zeros((total_rows, heads_dev), jnp.float32),
        jnp.full((total_rows, heads_dev), MASKED, jnp.float32),
    )
    numer_buf, denom_buf, peak_buf = lax.fori_loop(0, block_total, fill_block, initial)
    width = heads_dev * head_dim + 2 * heads_dev
    packed = jnp.concatenate([numer_buf, denom_buf, peak_buf], axis=1).reshape(
        blk_total, row_count * width
    )
    received = lax.all_to_all(packed, "blk", split_axis=0, concat_axis=0, tiled=True)
    received = received.reshape(blk_total, row_count, width)
    recv_numer = received[:, :, : heads_dev * head_dim]
    recv_denom = received[:, :, heads_dev * head_dim : heads_dev * head_dim + heads_dev]
    recv_peak = received[:, :, heads_dev * head_dim + heads_dev :]
    best = jnp.max(recv_peak, axis=0)
    factor = jnp.exp(recv_peak - best[None])
    summed_denom = jnp.sum(factor * recv_denom, axis=0)
    summed_numer = jnp.sum(
        recv_numer.reshape(blk_total, row_count, heads_dev, head_dim) * factor[:, :, :, None],
        axis=0,
    )
    attended = (summed_numer / summed_denom[:, :, None]).astype(jnp.bfloat16)
    mixed = jnp.einsum("rhd,hde->re", attended, out_fetched, preferred_element_type=jnp.float32)
    head_total = lax.axis_size("head")
    columns = mixed.shape[1] // head_total
    pieces = mixed.astype(jnp.bfloat16).reshape(row_count, head_total, columns)
    pieces = jnp.transpose(pieces, (1, 0, 2))
    exchanged = lax.all_to_all(pieces, "head", split_axis=0, concat_axis=0, tiled=True)
    summed = jnp.sum(exchanged.astype(jnp.float32), axis=0)
    bias_part = lax.dynamic_slice_in_dim(out_bias, lax.axis_index("head") * columns, columns, 0)
    return (summed + bias_part).astype(jnp.bfloat16)


def solution(mesh):
    return jax.shard_map(
        body,
        mesh=mesh,
        in_specs=(
            P("blk", None),
            P("blk", None),
            P(None, "blk", "head", None),
            P(),
            P(),
            P("blk", "head", None),
            P("head", None),
            P("head", "blk", None),
            P(),
            P(),
            P(),
            P(),
            P("blk"),
        ),
        out_specs=P("blk", "head"),
        check_vma=False,
    )
```

profile of v0, /device:TPU:8, one launch (start us, length us, event | category | flops | bytes accessed | tf_op | source)
XLA Modules:
  0.0 287.5 jit_solution(16090769834102768445)
XLA Ops:
  6.5 0.8 copy.52
  7.4 0.9 copy.51
  8.3 0.8 maximum_bitcast_fusion
  9.1 0.8 reduce-window.17
  9.9 0.8 reduce-window.18
  10.7 0.7 reduce.13
  11.6 1.4 fusion.49
  13.0 1.3 fusion.50
  14.3 0.6 concatenate.18
  15.0 0.6 concatenate.19
  15.6 0.7 broadcast_subtract_fusion
  16.3 3.2 %sort.17 = (s32[256]{0:T(256)}, s32[256]{0:T(256)S(1)}) sort(s32[256]{0:T(256)S(1)} %broadcast_subtract_fusion, s32[256]{0:T(256)S(1)} %iota.25), dimensions={0}, to_apply=%region_7.8 | sort | flops 2048 | bytes 4096 | tf_op jit(solution)/shard_map/jit(argsort)/sort | solution.py:51
  19.5 0.6 gather_fusion
  20.1 1.0 convert_reduce_fusion.1
  21.3 1.1 fusion.29
  22.4 0.2 fusion.23
  22.6 91.7 %all-gather.4.cloned.1.call-done = bf16[64,1,32768]{2,1,0:T(2,128)(2,1)} async-done(((bf16[1,1,32768]{2,1,0:T(2,128)(2,1)}), bf16[64,1,32768]{2,1,0:T(2,128)(2,1)}) %all-gather.4.cloned.1.call-update) | async-done | bytes 4194320 | tf_op jit(solution)/shard_map/all_gather | solution.py:57
  114.3 7.9 %copy.55 = bf16[64,1,32768]{2,0,1:T(8,128)(2,1)S(1)} copy(bf16[64,1,32768]{2,1,0:T(2,128)(2,1)} %all-gather.4.cloned.1.call-done) | data formatting | bytes 8388608
  122.2 1.9 copy-done.1
  124.2 1.9 slice.62
  126.0 4.8 %reshape_reshape.3 = bf16[2048,768]{1,0:T(8,128)(2,1)} reshape(bf16[64,24576]{1,0:T(8,128)(2,1)} %slice.62) | data formatting | bytes 6291456 | tf_op jit(solution)/shard_map/reshape;reshape | solution.py:65
  130.9 4.9 %reshape.221 = bf16[2048,1,768]{2,0,1:T(8,128)(2,1)} reshape(bf16[64,24576]{1,0:T(8,128)(2,1)} %slice.62) | data formatting | bytes 6291456 | tf_op jit(solution)/shard_map/reshape | solution.py:59
  135.8 2.6 fusion.19
  138.5 49.4 %all-gather = bf16[1536,1,256]{2,0,1:T(8,128)(2,1)S(1)} all-gather(bf16[24,1,256]{2,0,1:T(8,128)(2,1)S(1)} %get-tuple-element.212), channel_id=2, replica_groups=mesh['head'=8,'blk'=64] {'blk'}, dimensions={0}, use_global_device_ids=true | all-gather | bytes 798720 | tf_op jit(solution)/shard_map/all_gather | solution.py:81
  187.8 0.5 fusion.20
  188.4 0.8 scatter_custom_fusion
  189.2 1.0 scatter_custom_fusion.1
  190.2 0.7 pad_maximum_fusion.1
  190.9 0.6 broadcast_in_dim.64
  191.5 0.6 broadcast_in_dim.65
  192.1 11.9 %while.17 = (s32[]{:T(128)}, f32[1536,256]{1,0:T(8,128)S(1)}, f32[1536,1]{0,1:T(1,128)}, f32[1536,1]{0,1:T(1,128)}, s32[1536]{0:T(1024)}, /*index=5*/s32[280]{0:...) while((s32[]{:T(128)}, f32[1536,256]{1,0:T(8,128)S(1)}, ...), condition=%wide.region_15.16_spmd, body=%wide.region_12.15_spmd.sunk | while | flops 149380608 | bytes 2841579 | solution.py:134
  192.1 0.8 dynamic_slice.29
  192.9 1.0 select_reduce_fusion.2
  193.9 1.4 convolution_dynamic-update-slice_fusion.2
  195.3 0.2 fusion.60
  195.5 0.6 constant_dynamic-update-slice_fusion.3
  196.1 0.8 dynamic_slice.29
  196.8 1.0 select_reduce_fusion.2
  197.8 1.4 convolution_dynamic-update-slice_fusion.2
  199.4 0.6 constant_dynamic-update-slice_fusion.3
  200.0 0.8 dynamic_slice.29
  200.8 1.0 select_reduce_fusion.2
  201.8 1.4 convolution_dynamic-update-slice_fusion.2
  203.4 0.6 constant_dynamic-update-slice_fusion.3
  204.0 1.9 copy.40
  205.9 1.9 copy.39
  207.8 2.2 pad_maximum_fusion
  210.0 4.3 %all_to_all.12 = f32[64,1,6192]{2,1,0:T(1,128)} reshape(f32[1536,258]{1,0:T(8,128)S(1)} %pad_maximum_fusion) | data formatting | bytes 3170304 | tf_op jit(solution)/shard_map/all_to_all | solution.py:139
  214.3 10.0 %all-to-all-start = ((f32[64,1,6192]{2,1,0:T(1,128)}), f32[64,1,6192]{2,1,0:T(1,128)S(1)}, u32[]{:S(2)}, u32[]{:S(2)}) async-start(f32[64,1,6192]{2,1,0:T(1,128)} %all_to_all.12), calls=%async_computation | async-start | bytes 3211264 | tf_op jit(solution)/shard_map/all_to_all | solution.py:139
  224.3 2.3 slice.72
  226.6 2.7 reshape.225
  229.3 25.7 %all-to-all-done = f32[64,1,6192]{2,1,0:T(1,128)S(1)} async-done(((f32[64,1,6192]{2,1,0:T(1,128)}), f32[64,1,6192]{2,1,0:T(1,128)S(1)}, u32[]{:S(2)}, u32[]{:S(2)}) %all-to-all-start) | async-done | bytes 1585184 | tf_op jit(solution)/shard_map/all_to_all | solution.py:139
  255.0 5.4 %reduce.14 = f32[64,6192]{1,0:T(8,128)} reduce(f32[64,1,6192]{2,1,0:T(1,128)S(1)} %all-to-all-done, f32[]{:T(128)} %constant.108), dimensions={1}, to_apply=%all_to_all.10.reduce_sub_computation | reduce | bytes 3170308 | tf_op jit(solution)/shard_map/all_to_all | solution.py:139
  260.4 2.5 reshape.224
  262.9 1.5 fusion.51
  264.4 1.4 copy.48
  265.8 1.4 copy.47
  267.6 0.3 fusion.15
  267.8 1.5 convolution_convert_fusion
  269.3 0.7 copy.56
  270.0 4.3 %all-to-all-start.1 = ((bf16[8,24,256]{2,1,0:T(8,128)(2,1)}), bf16[8,24,256]{2,1,0:T(8,128)(2,1)S(1)}, u32[]{:S(2)}, u32[]{:S(2)}) async-start(bf16[8,24,256]{2,1,0:T(8,128)(2,1)} %bitcast.70), calls=%async_computation.1 | async-start | bytes 196608 | tf_op jit(solution)/shard_map/all_to_all | solution.py:157
  274.2 0.8 dynamic_slice.21
  275.0 5.0 %all-to-all-done.1 = bf16[8,24,256]{2,1,0:T(8,128)(2,1)S(1)} async-done(((bf16[8,24,256]{2,1,0:T(8,128)(2,1)}), bf16[8,24,256]{2,1,0:T(8,128)(2,1)S(1)}, u32[]{:S(2)}, u32[]{:S(2)}) %all-to-all-start.1) | async-done | bytes 98336 | tf_op jit(solution)/shard_map/all_to_all | solution.py:157
  280.1 0.6 add_convert_fusion
  (49 shorter events, 1.2 us)
Async XLA Ops:
  6.5 12.9 %copy-start = (bf16[256,2048]{1,0:T(8,128)(2,1)S(1)}, bf16[256,2048]{1,0:T(8,128)(2,1)}, u32[]{:S(2)}) copy-start(bf16[256,2048]{1,0:T(8,128)(2,1)} %param.16) | copy-start | bytes 3145732
  6.5 16.1 %copy-start.5 = (bf16[2,256,1,256]{3,1,2,0:T(8,128)(2,1)S(1)}, bf16[2,256,1,256]{3,1,2,0:T(8,128)(2,1)}, u32[]{:S(2)}) copy-start(bf16[2,256,1,256]{3,1,2,0:T(8,128)(2,1)} %param.17) | copy-start | bytes 786436
  6.5 107.8 %all-gather.4.cloned.1.call-start = ((), (), s32[]{:S(2)}) async-start(), calls=%async_computation.2 | async-start | bytes 8519680 | tf_op jit(solution)/shard_map/all_gather | solution.py:57
  11.5 1.5 copy-start.7
  122.2 1.9 copy-start.1
  130.9 4.9 %copy-start.4 = (bf16[24,2048]{1,0:T(8,128)(2,1)S(1)}, bf16[24,2048]{1,0:T(8,128)(2,1)}, u32[]{:S(2)}) copy-start(bf16[24,2048]{1,0:T(8,128)(2,1)} %param.15) | copy-start | bytes 294916
  130.9 4.9 %copy-start.8 = (f32[2048]{0:T(1024)S(1)}, f32[2048]{0:T(1024)}, u32[]{:S(2)}) copy-start(f32[2048]{0:T(1024)} %param.19) | copy-start | bytes 24580
  130.9 4.9 %copy-start.9 = (f32[2048]{0:T(1024)S(1)}, f32[2048]{0:T(1024)}, u32[]{:S(2)}) copy-start(f32[2048]{0:T(1024)} %param.18) | copy-start | bytes 24580
  135.8 52.0 %copy-start.3 = (bf16[2048,1,768]{2,0,1:T(8,128)(2,1)S(1)}, bf16[2048,1,768]{2,0,1:T(8,128)(2,1)}, u32[]{:S(2)}) copy-start(bf16[2048,1,768]{2,0,1:T(8,128)(2,1)} %reshape.221) | copy-start | bytes 9437188
  135.8 52.0 %slice-start = ((f32[1,768]{1,0:T(1,128)}), f32[1,512]{1,0:T(1,128)S(1)}, s32[]{:S(2)}) async-start(f32[1,768]{1,0:T(1,128)} %param.21), calls=%async_computation.3 | async-start | bytes 4096 | tf_op jit(solution)/shard_map/slice | solution.py:76
  192.1 3.1 %copy-start.6 = (s32[280]{0:T(512)S(1)}, s32[280]{0:T(512)}, u32[]{:S(2)}) copy-start(s32[280]{0:T(512)} %get-tuple-element.320) | copy-start | bytes 3364 | tf_op jit(solution)/shard_map/while
  196.1 3.1 %copy-start.6 = (s32[280]{0:T(512)S(1)}, s32[280]{0:T(512)}, u32[]{:S(2)}) copy-start(s32[280]{0:T(512)} %get-tuple-element.320) | copy-start | bytes 3364 | tf_op jit(solution)/shard_map/while
  200.0 3.2 %copy-start.6 = (s32[280]{0:T(512)S(1)}, s32[280]{0:T(512)}, u32[]{:S(2)}) copy-start(s32[280]{0:T(512)} %get-tuple-element.320) | copy-start | bytes 3364 | tf_op jit(solution)/shard_map/while
  204.0 3.8 %copy-start.2 = (f32[1536,256]{1,0:T(8,128)}, f32[1536,256]{1,0:T(8,128)S(1)}, u32[]{:S(2)}) copy-start(f32[1536,256]{1,0:T(8,128)S(1)} %get-tuple-element.178) | copy-start | bytes 4718596
  214.3 40.7 %all-to-all-start = ((f32[64,1,6192]{2,1,0:T(1,128)}), f32[64,1,6192]{2,1,0:T(1,128)S(1)}, u32[]{:S(2)}, u32[]{:S(2)}) async-start(f32[64,1,6192]{2,1,0:T(1,128)} %all_to_all.12), calls=%async_computation | async-start | bytes 3211264 | tf_op jit(solution)/shard_map/all_to_all | solution.py:139
  270.0 10.1 %all-to-all-start.1 = ((bf16[8,24,256]{2,1,0:T(8,128)(2,1)}), bf16[8,24,256]{2,1,0:T(8,128)(2,1)S(1)}, u32[]{:S(2)}, u32[]{:S(2)}) async-start(bf16[8,24,256]{2,1,0:T(8,128)(2,1)} %bitcast.70), calls=%async_computation.1 | async-start | bytes 196608 | tf_op jit(solution)/shard_map/all_to_all | solution.py:157
Sparse Core Ops, SparseCore 0:
  10.4 103.9 all-gather.3
where the time goes:
time: 289 us; the launch traced here: 288 us
  waiting for transfers between devices  122 us (42%)
  local copies, waits for them, and re-layouts  52.2 us (18%)
  blocking collectives  49.4 us (17%)
  other arithmetic  23.7 us (8%)
  starting transfers between devices  14.3 us (5%)
  between operations  13.6 us (5%)
  matrix products  11.7 us (4%)
    all_gather x1, waiting for transfers between devices, body(): fetched_all = lax.all_gather(packed_weights, 'blk', axis=0, tiled=True)  91.7 us
    all_gather x1, blocking collectives, body(): gathered = lax.all_gather(own_queries, 'blk', axis=0, tiled=True)  49.4 us
    all_to_all x1, waiting for transfers between devices, body(): lax.all_to_all(packed, 'blk', split_axis=0, concat_axis=0, tiled=True)  25.7 us
    unnamed x23, local copies, waits for them, and re-layouts  14.4 us
    all_to_all x1, starting transfers between devices, body(): lax.all_to_all(packed, 'blk', split_axis=0, concat_axis=0, tiled=True)  10 us
  transfers between devices with their start and end apart: 3, of which 3 were waited for; matrix products, arithmetic and copies ran while one was open for 7% of the time, Pallas kernels for 0%

commit v1 on v0

--- a/solution.py
+++ b/solution.py
@@ -78,7 +78,9 @@
         .reshape(FLAG_DEV, heads_dev, 2 * head_dim)
     )
     own_queries = projected[:, :, :head_dim].reshape(row_count, heads_dev * head_dim)
-    gathered = lax.all_gather(own_queries, "blk", axis=0, tiled=True)
+    gathered = jnp.concatenate(
+        lax.all_to_all(jnp.stack([own_queries] * lax.axis_size("blk")), "blk", 0, 0), axis=0
+    )
     prefix_keys = kv_cache[0].at[flagged].set(recomputed[:, :, :head_dim])
     prefix_values = kv_cache[1].at[flagged].set(recomputed[:, :, head_dim:])
     keys_all = jnp.concatenate([prefix_keys, projected[:, :, head_dim : 2 * head_dim]], axis=0)

time: 289 us -> 274 us (0.948)
  the two profiles are of different devices: /device:TPU:8 before, /device:TPU:1 now
where the time goes in v1:
time: 274 us; the launch traced here: 273 us
  waiting for transfers between devices  142 us (52%)
  local copies, waits for them, and re-layouts  53.1 us (19%)
  starting transfers between devices  27.6 us (10%)
  other arithmetic  23.7 us (9%)
  between operations  13.6 us (5%)
  matrix products  13.2 us (5%)
    all_gather x1, waiting for transfers between devices, body(): fetched_all = lax.all_gather(packed_weights, 'blk', axis=0, tiled=True)  93.7 us
    all_to_all x1, waiting for transfers between devices, body(): lax.all_to_all(packed, 'blk', split_axis=0, concat_axis=0, tiled=True)  32.9 us
    unnamed x21, local copies, waits for them, and re-layouts  14.4 us
    all_to_all x1, waiting for transfers between devices, body(): lax.all_to_all(jnp.stack([own_queries] * lax.axis_size('blk')), 'blk', 0, 0)  10.7 us
    all_to_all x1, starting transfers between devices, body(): lax.all_to_all(jnp.stack([own_queries] * lax.axis_size('blk')), 'blk', 0, 0)  9.79 us
    all_to_all x1, starting transfers between devices, body(): lax.all_to_all(packed, 'blk', split_axis=0, concat_axis=0, tiled=True)  9.26 us
    all_to_all x1, starting transfers between devices, body(): lax.all_to_all(pieces, 'head', split_axis=0, concat_axis=0, tiled=True)  8.58 us
  transfers between devices with their start and end apart: 4, of which 4 were waited for; matrix products, arithmetic and copies ran while one was open for 10% of the time, Pallas kernels for 0%

profile of v1, /device:TPU:1, one launch (start us, length us, event | category | flops | bytes accessed | tf_op | source)
XLA Modules:
  0.0 272.9 jit_solution(16990334677357716392)
XLA Ops:
  6.5 0.8 copy.52
  7.4 0.9 copy.51
  8.3 0.8 maximum_bitcast_fusion
  9.1 0.8 reduce-window.17
  9.9 0.8 reduce-window.18
  10.7 0.7 reduce.13
  11.6 1.4 fusion.49
  13.0 1.3 fusion.50
  14.3 0.6 concatenate.18
  15.0 0.6 concatenate.19
  15.6 0.7 broadcast_subtract_fusion
  16.2 3.2 %sort.17 = (s32[256]{0:T(256)}, s32[256]{0:T(256)S(1)}) sort(s32[256]{0:T(256)S(1)} %broadcast_subtract_fusion, s32[256]{0:T(256)S(1)} %iota.25), dimensions={0}, to_apply=%region_7.8 | sort | flops 2048 | bytes 4096 | tf_op jit(solution)/shard_map/jit(argsort)/sort | solution.py:51
  19.4 1.0 convert_reduce_fusion.1
  20.5 1.1 fusion.29
  21.6 93.7 %all-gather.3.cloned.1.call-done = bf16[64,1,32768]{2,1,0:T(2,128)(2,1)} async-done(((bf16[1,1,32768]{2,1,0:T(2,128)(2,1)}), bf16[64,1,32768]{2,1,0:T(2,128)(2,1)}) %all-gather.3.cloned.1.call-update) | async-done | bytes 4194320 | tf_op jit(solution)/shard_map/all_gather | solution.py:57
  115.2 7.9 %copy.55 = bf16[64,1,32768]{2,0,1:T(8,128)(2,1)S(1)} copy(bf16[64,1,32768]{2,1,0:T(2,128)(2,1)} %all-gather.3.cloned.1.call-done) | data formatting | bytes 8388608
  123.2 1.9 copy-done.1
  125.1 1.9 slice.62
  127.0 4.9 %reshape_reshape.3 = bf16[2048,768]{1,0:T(8,128)(2,1)} reshape(bf16[64,24576]{1,0:T(8,128)(2,1)} %slice.62) | data formatting | bytes 6291456 | tf_op jit(solution)/shard_map/reshape;reshape | solution.py:65
  131.8 2.5 fusion.19
  134.3 0.9 stack.3
  135.3 9.8 %all-to-all-start = ((bf16[64,24,256]{2,1,0:T(8,128)(2,1)}), bf16[64,24,256]{2,1,0:T(8,128)(2,1)S(1)}, u32[]{:S(2)}, u32[]{:S(2)}) async-start(bf16[64,24,256]{2,1,0:T(8,128)(2,1)} %stack.3), calls=%async_computation | async-start | bytes 1572864 | tf_op jit(solution)/shard_map/all_to_all | solution.py:82
  145.1 0.6 gather_fusion
  146.1 4.8 %reshape.223 = bf16[2048,1,768]{2,0,1:T(8,128)(2,1)} reshape(bf16[64,24576]{1,0:T(8,128)(2,1)} %slice.62) | data formatting | bytes 6291456 | tf_op jit(solution)/shard_map/reshape | solution.py:59
  151.0 2.1 fusion.20
  153.1 0.8 scatter_custom_fusion
  153.9 1.0 scatter_custom_fusion.1
  154.9 0.7 pad_maximum_fusion.1
  155.6 10.7 %all-to-all-done = bf16[64,24,256]{2,1,0:T(8,128)(2,1)S(1)} async-done(((bf16[64,24,256]{2,1,0:T(8,128)(2,1)}), bf16[64,24,256]{2,1,0:T(8,128)(2,1)S(1)}, u32[]{:S(2)}, u32[]{:S(2)}) %all-to-all-start) | async-done | bytes 786464 | tf_op jit(solution)/shard_map/all_to_all | solution.py:82
  166.3 0.6 broadcast_in_dim.64
  166.9 0.6 broadcast_in_dim.65
  167.5 11.9 %while.17 = (s32[]{:T(128)}, f32[1536,256]{1,0:T(8,128)S(1)}, f32[1536,1]{0,1:T(1,128)}, f32[1536,1]{0,1:T(1,128)}, s32[1536]{0:T(1024)}, /*index=5*/s32[280]{0:...) while((s32[]{:T(128)}, f32[1536,256]{1,0:T(8,128)S(1)}, ...), condition=%wide.region_15.16_spmd, body=%wide.region_12.15_spmd.sunk | while | flops 149380608 | bytes 2841579 | solution.py:136
  167.6 0.8 dynamic_slice.29
  168.3 1.0 select_reduce_fusion.2
  169.3 1.4 convolution_dynamic-update-slice_fusion.2
  170.9 0.6 constant_dynamic-update-slice_fusion.3
  171.5 0.8 dynamic_slice.29
  172.3 1.0 select_reduce_fusion.2
  173.3 1.4 convolution_dynamic-update-slice_fusion.2
  174.8 0.6 constant_dynamic-update-slice_fusion.3
  175.5 0.8 dynamic_slice.29
  176.2 1.0 select_reduce_fusion.2
  177.2 1.4 convolution_dynamic-update-slice_fusion.2
  178.8 0.6 constant_dynamic-update-slice_fusion.3
  179.4 1.9 copy.40
  181.3 1.9 copy.39
  183.2 2.2 pad_maximum_fusion
  185.4 4.3 %all_to_all.16 = f32[64,1,6192]{2,1,0:T(1,128)} reshape(f32[1536,258]{1,0:T(8,128)S(1)} %pad_maximum_fusion) | data formatting | bytes 3170304 | tf_op jit(solution)/shard_map/all_to_all | solution.py:141
  189.7 9.3 %all-to-all-start.1 = ((f32[64,1,6192]{2,1,0:T(1,128)}), f32[64,1,6192]{2,1,0:T(1,128)S(1)}, u32[]{:S(2)}, u32[]{:S(2)}) async-start(f32[64,1,6192]{2,1,0:T(1,128)} %all_to_all.16), calls=%async_computation.1 | async-start | bytes 3211264 | tf_op jit(solution)/shard_map/all_to_all | solution.py:141
  199.0 2.3 slice.72
  201.2 2.7 reshape.227
  203.9 32.9 %all-to-all-done.1 = f32[64,1,6192]{2,1,0:T(1,128)S(1)} async-done(((f32[64,1,6192]{2,1,0:T(1,128)}), f32[64,1,6192]{2,1,0:T(1,128)S(1)}, u32[]{:S(2)}, u32[]{:S(2)}) %all-to-all-start.1) | async-done | bytes 1585184 | tf_op jit(solution)/shard_map/all_to_all | solution.py:141
  236.9 5.4 %reduce.14 = f32[64,6192]{1,0:T(8,128)} reduce(f32[64,1,6192]{2,1,0:T(1,128)S(1)} %all-to-all-done.1, f32[]{:T(128)} %constant.108), dimensions={1}, to_apply=%all_to_all.14.reduce_sub_computation | reduce | bytes 3170308 | tf_op jit(solution)/shard_map/all_to_all | solution.py:141
  242.2 2.5 reshape.226
  244.8 1.5 fusion.51
  246.3 1.4 copy.48
  247.7 1.4 copy.47
  249.4 0.3 fusion.15
  249.7 1.5 convolution_convert_fusion
  251.2 0.7 copy.56
  251.9 8.6 %all-to-all-start.2 = ((bf16[8,24,256]{2,1,0:T(8,128)(2,1)}), bf16[8,24,256]{2,1,0:T(8,128)(2,1)S(1)}, u32[]{:S(2)}, u32[]{:S(2)}) async-start(bf16[8,24,256]{2,1,0:T(8,128)(2,1)} %bitcast.72), calls=%async_computation.2 | async-start | bytes 196608 | tf_op jit(solution)/shard_map/all_to_all | solution.py:159
  260.5 0.8 dynamic_slice.21
  261.2 4.2 %all-to-all-done.2 = bf16[8,24,256]{2,1,0:T(8,128)(2,1)S(1)} async-done(((bf16[8,24,256]{2,1,0:T(8,128)(2,1)}), bf16[8,24,256]{2,1,0:T(8,128)(2,1)S(1)}, u32[]{:S(2)}, u32[]{:S(2)}) %all-to-all-start.2) | async-done | bytes 98336 | tf_op jit(solution)/shard_map/all_to_all | solution.py:159
  265.5 0.6 add_convert_fusion
  (49 shorter events, 1.6 us)
Async XLA Ops:
  6.5 138.6 %copy-start = (bf16[256,2048]{1,0:T(8,128)(2,1)S(1)}, bf16[256,2048]{1,0:T(8,128)(2,1)}, u32[]{:S(2)}) copy-start(bf16[256,2048]{1,0:T(8,128)(2,1)} %param.16) | copy-start | bytes 3145732
  6.5 108.7 %all-gather.3.cloned.1.call-start = ((), (), s32[]{:S(2)}) async-start(), calls=%async_computation.3 | async-start | bytes 8519680 | tf_op jit(solution)/shard_map/all_gather | solution.py:57
  11.5 1.5 copy-start.6
  123.1 1.9 copy-start.1
  127.0 4.9 %copy-start.3 = (bf16[24,2048]{1,0:T(8,128)(2,1)S(1)}, bf16[24,2048]{1,0:T(8,128)(2,1)}, u32[]{:S(2)}) copy-start(bf16[24,2048]{1,0:T(8,128)(2,1)} %param.15) | copy-start | bytes 294916
  127.0 4.9 %copy-start.7 = (f32[2048]{0:T(1024)S(1)}, f32[2048]{0:T(1024)}, u32[]{:S(2)}) copy-start(f32[2048]{0:T(1024)} %param.19) | copy-start | bytes 24580
  127.0 4.9 %copy-start.8 = (f32[2048]{0:T(1024)S(1)}, f32[2048]{0:T(1024)}, u32[]{:S(2)}) copy-start(f32[2048]{0:T(1024)} %param.18) | copy-start | bytes 24580
  134.3 11.8 %copy-start.4 = (bf16[2,256,1,256]{3,1,2,0:T(8,128)(2,1)S(1)}, bf16[2,256,1,256]{3,1,2,0:T(8,128)(2,1)}, u32[]{:S(2)}) copy-start(bf16[2,256,1,256]{3,1,2,0:T(8,128)(2,1)} %param.17) | copy-start | bytes 786436
  135.3 31.0 %all-to-all-start = ((bf16[64,24,256]{2,1,0:T(8,128)(2,1)}), bf16[64,24,256]{2,1,0:T(8,128)(2,1)S(1)}, u32[]{:S(2)}, u32[]{:S(2)}) async-start(bf16[64,24,256]{2,1,0:T(8,128)(2,1)} %stack.3), calls=%async_computation | async-start | bytes 1572864 | tf_op jit(solution)/shard_map/all_to_all | solution.py:82
  146.1 4.8 %slice-start = ((f32[1,768]{1,0:T(1,128)}), f32[1,512]{1,0:T(1,128)S(1)}, s32[]{:S(2)}) async-start(f32[1,768]{1,0:T(1,128)} %param.21), calls=%async_computation.4 | async-start | bytes 4096 | tf_op jit(solution)/shard_map/slice | solution.py:76
  167.5 3.1 %copy-start.5 = (s32[280]{0:T(512)S(1)}, s32[280]{0:T(512)}, u32[]{:S(2)}) copy-start(s32[280]{0:T(512)} %get-tuple-element.320) | copy-start | bytes 3364 | tf_op jit(solution)/shard_map/while
  171.5 3.1 %copy-start.5 = (s32[280]{0:T(512)S(1)}, s32[280]{0:T(512)}, u32[]{:S(2)}) copy-start(s32[280]{0:T(512)} %get-tuple-element.320) | copy-start | bytes 3364 | tf_op jit(solution)/shard_map/while
  175.4 3.1 %copy-start.5 = (s32[280]{0:T(512)S(1)}, s32[280]{0:T(512)}, u32[]{:S(2)}) copy-start(s32[280]{0:T(512)} %get-tuple-element.320) | copy-start | bytes 3364 | tf_op jit(solution)/shard_map/while
  179.4 3.8 %copy-start.2 = (f32[1536,256]{1,0:T(8,128)}, f32[1536,256]{1,0:T(8,128)S(1)}, u32[]{:S(2)}) copy-start(f32[1536,256]{1,0:T(8,128)S(1)} %get-tuple-element.178) | copy-start | bytes 4718596
  189.7 47.2 %all-to-all-start.1 = ((f32[64,1,6192]{2,1,0:T(1,128)}), f32[64,1,6192]{2,1,0:T(1,128)S(1)}, u32[]{:S(2)}, u32[]{:S(2)}) async-start(f32[64,1,6192]{2,1,0:T(1,128)} %all_to_all.16), calls=%async_computation.1 | async-start | bytes 3211264 | tf_op jit(solution)/shard_map/all_to_all | solution.py:141
  251.9 13.6 %all-to-all-start.2 = ((bf16[8,24,256]{2,1,0:T(8,128)(2,1)}), bf16[8,24,256]{2,1,0:T(8,128)(2,1)S(1)}, u32[]{:S(2)}, u32[]{:S(2)}) async-start(bf16[8,24,256]{2,1,0:T(8,128)(2,1)} %bitcast.72), calls=%async_computation.2 | async-start | bytes 196608 | tf_op jit(solution)/shard_map/all_to_all | solution.py:159
Sparse Core Ops, SparseCore 0:
  10.4 104.8 all-gather.2
